TPU v7x, 32 devices: a whole 2x2x4 slice. The times are simulated.
32 devices in a mesh: seq: 16 (over z, y, core), head: 2 (over x).
Axes of the slice: x: 2, y: 2, z: 4, core: 2. Of those that a mesh axis runs over, the one named last changes fastest.
Arguments:
- tokens: bfloat16 [8192, 5120], P(('seq', 'head')), may hold values from -6 to 6
- w_qkv: bfloat16 [3, 5120, 640], P(None, None, 'head'), may hold values from -0.078125 to 0.078125
- scale_exp: int32 [3, 40, 2], P(None, None, 'head'), may hold values from -2 to 1
- gate_mask: int32 [8192, 2], P('seq', 'head'), may hold values 0 or 1
- rate: float32 [2], P('head'), may hold values from 0.00044194172 to 0.0022097088
- fast_gate: bfloat16 [2, 320, 640], P('head'), may hold values from -0.3125 to 0.3125
- fast_up: bfloat16 [2, 320, 640], P('head'), may hold values from -0.3125 to 0.3125
- fast_down: bfloat16 [2, 320, 640], P('head'), may hold values from -0.25 to 0.25
Outputs:
- answers: bfloat16 [8192, 640], P(('seq', 'head'))
All inputs are finite; a program needn't handle non-finite values. No bound on the sum of `gate_mask` on one device may be relied on, other than what follows from the above.
Results may differ from a plain program's by a relative error of at most 0.012.
Values may be sent and summed in bfloat16 or wider, within the bound.
A program may use at most 64 MiB of HBM per device.

v0:
```python
import jax
import jax.numpy as jnp
from jax import lax
from jax.sharding import PartitionSpec as P


def local_grads(keys, values, weight, old):
    gate = jnp.dot(keys, old[0], preferred_element_type=jnp.float32)
    upper = jnp.dot(keys, old[1], preferred_element_type=jnp.float32)
    sigma = jax.nn.sigmoid(gate)
    active = gate * sigma
    hidden = (active * upper).astype(jnp.bfloat16)
    weighted = (weight[:, None] * values.astype(jnp.float32)).astype(jnp.bfloat16)
    d_hidden = jnp.dot(weighted, old[2], preferred_element_type=jnp.float32)
    d_gate = (d_hidden * upper * sigma * (1.0 + gate * (1.0 - sigma))).astype(jnp.bfloat16)
    d_upper = (d_hidden * active).astype(jnp.bfloat16)
    dims = (((0,), (0,)), ((), ()))
    grad_gate = lax.dot_general(keys, d_gate, dims, preferred_element_type=jnp.float32)
    grad_upper = lax.dot_general(keys, d_upper, dims, preferred_element_type=jnp.float32)
    grad_down = lax.dot_general(weighted, hidden, dims, preferred_element_type=jnp.float32)
    return jnp.stack([grad_gate, grad_upper, grad_down])


def respond(query, renorm):
    gate = jnp.dot(query, renorm[0], preferred_element_type=jnp.float32)
    upper = jnp.dot(query, renorm[1], preferred_element_type=jnp.float32)
    hidden = (jax.nn.silu(gate) * upper).astype(jnp.bfloat16)
    output = lax.dot_general(
        hidden, renorm[2], (((1,), (1,)), ((), ())), preferred_element_type=jnp.float32
    )
    scaled = output * lax.rsqrt(jnp.mean(output * output, axis=-1, keepdims=True) + 1e-05)
    return scaled.astype(jnp.bfloat16)


def body(tokens, w_qkv, scale_exp, gate_mask, rate, fast_gate, fast_up, fast_down):
    factor = jnp.exp2(scale_exp.astype(jnp.float32))[:, :, 0]
    block_rows = w_qkv.shape[1] // factor.shape[1]
    factor = jnp.repeat(factor, block_rows, axis=1)[:, :, None].astype(jnp.bfloat16)
    weff = w_qkv * factor
    triple = jnp.einsum(
        "rd,cdh->rch",
        lax.all_gather(tokens, "head", axis=0, tiled=True),
        weff,
        preferred_element_type=jnp.float32,
    ).astype(jnp.bfloat16)
    query = triple[:, 0]
    keys = triple[:, 1]
    values = triple[:, 2]
    weight = rate[0] * gate_mask[:, 0].astype(jnp.float32)
    old = jnp.stack([fast_gate[0], fast_up[0], fast_down[0]])
    partial_grads = local_grads(keys, values, weight, old)
    old_f = old.astype(jnp.float32)
    old_norm = jnp.sqrt(jnp.sum(old_f * old_f, axis=1))
    total = lax.psum(partial_grads, "seq")
    fresh = old_f + total
    new_sq = jnp.sum(fresh * fresh, axis=1)
    renorm = (fresh * (old_norm / jnp.sqrt(new_sq + 1e-06))[:, None, :]).astype(jnp.bfloat16)
    answer = respond(query, renorm)
    return lax.all_to_all(answer, "head", split_axis=0, concat_axis=1, tiled=True)


def solution(mesh):
    in_specs = (
        P(("seq", "head"), None),
        P(None, None, "head"),
        P(None, None, "head"),
        P("seq", "head"),
        P("head"),
        P("head", None, None),
        P("head", None, None),
        P("head", None, None),
    )
    out_specs = P(("seq", "head"), None)
    return jax.shard_map(body, mesh=mesh, in_specs=in_specs, out_specs=out_specs, check_vma=False)
```

profile of v0, /device:TPU:0, one launch (start us, length us, event | category | flops | bytes accessed | tf_op | source)
XLA Modules:
  0.0 218.8 jit_solution(169645211959964053)
XLA Ops:
  6.5 0.0 copy-start.5
  6.5 0.0 copy-start.4
  6.5 0.0 all-gather.2.cloned.1.call-start
  6.5 0.7 all-gather.2.cloned.1.call-update
  7.3 0.0 all-reduce.2.cloned.1.call-start
  8.0 0.0 copy-done.5
  8.0 0.1 broadcast_bitcast_fusion
  8.1 0.0 copy-done.4
  8.1 72.0 %all-gather.2.cloned.1.call-done = bf16[512,5120]{1,0:T(8,128)(2,1)} async-done(((bf16[256,5120]{1,0:T(8,128)(2,1)}), bf16[512,5120]{1,0:T(8,128)(2,1)}) %all-gather.2.cloned.1.call-update) | async-done | bytes 5242896 | tf_op jit(solution)/shard_map/all_gather | solution.py:42
  80.2 0.0 copy-start.2
  80.2 9.5 %fusion.10 = bf16[512,3,320]{0,2,1:T(8,128)(2,1)S(1)} fusion(bf16[512,5120]{1,0:T(8,128)(2,1)} %all-gather.2.cloned.1.call-done, bf16[3,5120,320]{1,2,0:T(8,128)(2,1)} %param.9, bf16[3,5120]{1,0:T(4,128)(2,1)S(1)} %bitcast.82), kind=kOutput, calls=%fused_computation.12 | convolution fusion | flops 5038571520 | bytes 16087040 | tf_op jit(solution)/shard_map/rd,cdh->rch/dot_general | solution.py:40
  89.7 0.0 copy-done.2
  89.7 0.0 copy-start.1
  89.7 0.6 fusion.23
  90.3 0.4 copy-done.1
  90.7 0.6 fusion.25
  91.3 0.4 copy-done.3
  91.7 0.6 fusion.27
  92.3 0.6 convolution_bitcast_fusion.1
  92.9 0.8 convolution_bitcast_fusion.2
  93.7 0.6 convolution_bitcast_fusion
  94.3 1.6 pad_maximum_fusion
  95.9 0.0 all-reduce.2.cloned.1.call-update
  96.0 100.3 %all-reduce.2.cloned.1.call-done = f32[3,320,640]{2,1,0:T(8,128)} async-done(((f32[3,320,640]{2,1,0:T(8,128)}), f32[3,320,640]{2,1,0:T(8,128)}) %all-reduce.2.cloned.1.call-update) | async-done | bytes 2457616 | tf_op jit(solution)/shard_map/psum | solution.py:54
  196.2 2.4 %fusion.4 = (f32[3,640]{1,0:T(4,128)S(1)}, f32[3,640]{1,0:T(4,128)S(1)}) fusion(bf16[1,320,640]{2,1,0:T(8,128)(2,1)S(1)} %copy-done.3, bf16[1,320,640]{2,1,0:T(8,128)(2,1)S(1)} %copy-done.1, bf16[1,320,640]{2,1,0:T(8,128)(2,1)S(1)} %copy-done.2, f32[3,320,640]{2,1,0:T(8,128)} %all-reduce.2.cloned.1.call-done), kind=kLoop, calls=%fused_computation.6 | loop fusion | flops 4911360 | bytes 3701760 | tf_op jit(solution)/shard_map/reduce_sum | solution.py:53
  198.6 0.1 copy-done
  198.7 0.4 multiply_convert_fusion
  199.0 1.6 fusion.22
  200.7 2.3 %multiply_reduce_fusion.1 = (f32[512]{0:T(512)S(1)}, f32[512,320]{0,1:T(8,128)S(1)}) fusion(bf16[3,320,640]{2,1,0:T(8,128)(2,1)S(1)} %multiply_convert_fusion, f32[512,640]{1,0:T(8,128)} %fusion.22, bf16[512,3,320]{0,2,1:T(8,128)(2,1)S(1)} %fusion.10), kind=kOutput, calls=%fused_computation.30 | convolution fusion | flops 421723648 | bytes 3115008 | tf_op jit(solution)/shard_map/dot_general | solution.py:28
  203.0 0.1 multiply_convert_fusion.6
  203.1 7.9 %all_to_all.19 = bf16[2,256,320]{1,2,0:T(8,128)(2,1)S(1)} all-to-all(bf16[2,256,320]{1,2,0:T(8,128)(2,1)S(1)} %bitcast.79), channel_id=1, replica_groups=mesh['seq'=16,'head'=2] {'head'}, dimensions={0} | all-to-all | bytes 655360 | tf_op jit(solution)/shard_map/all_to_all | solution.py:59
  211.1 0.9 copy.11
  (9 shorter events, 0.1 us)
Async XLA Ops:
  6.5 1.4 copy-start.5
  6.5 1.6 copy-start.4
  6.5 73.6 %all-gather.2.cloned.1.call-start = ((), (), s32[]{:S(2)}) async-start(), calls=%async_computation.1 | async-start | bytes 7864320 | tf_op jit(solution)/shard_map/all_gather | solution.py:42
  7.3 189.0 %all-reduce.2.cloned.1.call-start = ((), (), s32[]{:S(2)}) async-start(), calls=%async_computation.2 | async-start | bytes 4915200 | tf_op jit(solution)/shard_map/psum | solution.py:54
  80.2 9.5 %copy-start.2 = (bf16[1,320,640]{2,1,0:T(8,128)(2,1)S(1)}, bf16[1,320,640]{2,1,0:T(8,128)(2,1)}, u32[]{:S(2)}) copy-start(bf16[1,320,640]{2,1,0:T(8,128)(2,1)} %param.13) | copy-start | bytes 1228804
  89.7 1.0 copy-start.1
  90.7 1.0 copy-start.3
  196.2 2.4 %copy-start = (f32[3,320,640]{2,1,0:T(8,128)S(1)}, f32[3,320,640]{2,1,0:T(8,128)}, u32[]{:S(2)}) copy-start(f32[3,320,640]{2,1,0:T(8,128)} %all-reduce.2.cloned.1.call-done) | copy-start | bytes 7372804
Sparse Core Ops, SparseCore 0:
  8.9 71.2 all-gather.1
  96.1 100.1 all-reduce.1
where the time goes:
time: 219 us
  waiting for transfers between devices  173 us (79%)
  matrix products  17.3 us (8%)
  between operations  14.2 us (6%)
  blocking collectives  7.95 us (4%)
  other arithmetic  4.41 us (2%)
    psum x1, waiting for transfers between devices, body(): total = lax.psum(partial_grads, 'seq')  100 us
    all_gather x1, waiting for transfers between devices, body(): lax.all_gather(tokens, 'head', axis=0, tiled=True)  72 us
    dot_general x1, matrix products, body(): jnp.einsum('rd,cdh->rch', lax.all_gather(tokens, 'head', axis=0, tiled=Tr...  9.51 us
    all_to_all x1, blocking collectives, body(): lax.all_to_all(answer, 'head', split_axis=0, concat_axis=1, tiled=True)  7.95 us
  transfers between devices with their start and end apart: 2, of which 2 were waited for; matrix products, arithmetic and copies ran while one was open for 0% of the time, Pallas kernels for 0%

commit v1 on v0

--- a/solution.py
+++ b/solution.py
@@ -51,7 +51,7 @@
     partial_grads = local_grads(keys, values, weight, old)
     old_f = old.astype(jnp.float32)
     old_norm = jnp.sqrt(jnp.sum(old_f * old_f, axis=1))
-    total = lax.psum(partial_grads, "seq")
+    total = jnp.sum(lax.all_gather(partial_grads, axis_name="seq"), 0)
     fresh = old_f + total
     new_sq = jnp.sum(fresh * fresh, axis=1)
     renorm = (fresh * (old_norm / jnp.sqrt(new_sq + 1e-06))[:, None, :]).astype(jnp.bfloat16)

time: 219 us -> 330 us (1.51)
  waiting for transfers between devices: 173 us -> 268 us
  other arithmetic: 4.41 us -> 17.5 us
    all_gather x0 -> x1, waiting for transfers between devices: none -> 195 us  [body(): total = jnp.sum(lax.all_gather(partial_grads, axis_name='seq'), 0)]
    psum x1 -> x0, waiting for transfers between devices: 100 us -> none  [body(): total = lax.psum(partial_grads, 'seq')]
    reduce_sum x0 -> x1, other arithmetic: none -> 13.9 us  [body(): total = jnp.sum(lax.all_gather(partial_grads, axis_name='seq'), 0)]
where the time goes in v1:
time: 330 us; the launch traced here: 329 us
  waiting for transfers between devices  268 us (81%)
  other arithmetic  17.5 us (5%)
  matrix products  17.2 us (5%)
  between operations  14.3 us (4%)
  blocking collectives  8.96 us (3%)
    all_gather x1, waiting for transfers between devices, body(): total = jnp.sum(lax.all_gather(partial_grads, axis_name='seq'), 0)  195 us
    all_gather x1, waiting for transfers between devices, body(): lax.all_gather(tokens, 'head', axis=0, tiled=True)  72 us
    reduce_sum x1, other arithmetic, body(): total = jnp.sum(lax.all_gather(partial_grads, axis_name='seq'), 0)  13.9 us
    dot_general x1, matrix products, body(): jnp.einsum('rd,cdh->rch', lax.all_gather(tokens, 'head', axis=0, tiled=Tr...  9.51 us
    all_to_all x1, blocking collectives, body(): lax.all_to_all(answer, 'head', split_axis=0, concat_axis=1, tiled=True)  8.96 us
  transfers between devices with their start and end apart: 2, of which 2 were waited for; matrix products, arithmetic and copies ran while one was open for 0% of the time, Pallas kernels for 0%

profile of v1, /device:TPU:0, one launch (start us, length us, event | category | flops | bytes accessed | tf_op | source)
XLA Modules:
  0.0 329.2 jit_solution(3879309964370882839)
XLA Ops:
  6.5 0.0 all-gather.4.cloned.1.call-start
  6.5 0.7 all-gather.4.cloned.1.call-update
  7.3 0.0 all-gather.6.cloned.1.call-start
  8.0 0.0 copy-done.7
  8.0 0.1 broadcast_bitcast_fusion
  8.1 0.0 copy-done.6
  8.1 72.0 %all-gather.4.cloned.1.call-done = bf16[512,5120]{1,0:T(8,128)(2,1)} async-done(((bf16[256,5120]{1,0:T(8,128)(2,1)}), bf16[512,5120]{1,0:T(8,128)(2,1)}) %all-gather.4.cloned.1.call-update) | async-done | bytes 5242896 | tf_op jit(solution)/shard_map/all_gather | solution.py:42
  80.2 9.5 %fusion.10 = bf16[512,3,320]{0,2,1:T(8,128)(2,1)S(1)} fusion(bf16[512,5120]{1,0:T(8,128)(2,1)} %all-gather.4.cloned.1.call-done, bf16[3,5120,320]{1,2,0:T(8,128)(2,1)} %param.9, bf16[3,5120]{1,0:T(4,128)(2,1)S(1)} %bitcast.84), kind=kOutput, calls=%fused_computation.12 | convolution fusion | flops 5038571520 | bytes 16087040 | tf_op jit(solution)/shard_map/rd,cdh->rch/dot_general | solution.py:40
  89.7 0.0 copy-start
  89.7 0.6 fusion.23
  90.3 0.7 copy-done
  91.0 0.6 fusion.25
  91.6 0.4 copy-done.2
  92.0 0.6 fusion.27
  92.6 0.6 convolution_bitcast_fusion.1
  93.2 0.8 convolution_bitcast_fusion.2
  94.0 0.0 copy-done.5
  94.0 0.7 convolution_bitcast_fusion
  94.7 1.6 pad_maximum_fusion
  96.2 0.0 all-gather.6.cloned.1.call-update
  96.3 195.4 %all-gather.6.cloned.1.call-done = f32[48,320,640]{2,1,0:T(8,128)} async-done(((f32[3,320,640]{2,1,0:T(8,128)}), f32[48,320,640]{2,1,0:T(8,128)}) %all-gather.6.cloned.1.call-update) | async-done | bytes 39321616 | tf_op jit(solution)/shard_map/all_gather | solution.py:54
  291.6 13.9 %reduce_sum.36 = f32[3,320,640]{2,1,0:T(8,128)S(1)} reduce(f32[16,3,320,640]{3,2,1,0:T(8,128)} %bitcast.80, f32[]{:T(128)} %constant.3.clone.1), dimensions={0}, to_apply=%region_0.0 | reduce | flops 9216000 | bytes 41779204 | tf_op jit(solution)/shard_map/reduce_sum | solution.py:54
  305.6 0.0 copy-start.3
  305.6 1.6 fusion.4
  307.2 0.3 multiply_convert_fusion
  307.5 0.0 copy-start.4
  307.5 1.0 copy-done.4
  308.6 1.5 fusion.22
  310.1 2.3 multiply_reduce_fusion.1
  312.4 0.1 multiply_convert_fusion.6
  312.5 9.0 %all_to_all.19 = bf16[2,256,320]{1,2,0:T(8,128)(2,1)S(1)} all-to-all(bf16[2,256,320]{1,2,0:T(8,128)(2,1)S(1)} %bitcast.81), channel_id=1, replica_groups=mesh['seq'=16,'head'=2] {'head'}, dimensions={0} | all-to-all | bytes 655360 | tf_op jit(solution)/shard_map/all_to_all | solution.py:59
  321.5 0.9 copy.13
  (14 shorter events, 0.1 us)
Async XLA Ops:
  6.5 1.4 copy-start.7
  6.5 1.6 copy-start.6
  6.5 73.6 %all-gather.4.cloned.1.call-start = ((), (), s32[]{:S(2)}) async-start(), calls=%async_computation.1 | async-start | bytes 7864320 | tf_op jit(solution)/shard_map/all_gather | solution.py:42
  7.3 284.4 %all-gather.6.cloned.1.call-start = ((), (), s32[]{:S(2)}) async-start(), calls=%async_computation.2 | async-start | bytes 41779200 | tf_op jit(solution)/shard_map/all_gather | solution.py:54
  80.2 9.5 %copy-start.1 = (bf16[1,320,640]{2,1,0:T(8,128)(2,1)S(1)}, bf16[1,320,640]{2,1,0:T(8,128)(2,1)}, u32[]{:S(2)}) copy-start(bf16[1,320,640]{2,1,0:T(8,128)(2,1)} %param.13) | copy-start | bytes 1228804
  89.7 4.3 %copy-start.5 = (bf16[512,3,320]{0,2,1:T(8,128)(2,1)}, bf16[512,3,320]{0,2,1:T(8,128)(2,1)S(1)}, u32[]{:S(2)}) copy-start(bf16[512,3,320]{0,2,1:T(8,128)(2,1)S(1)} %fusion.10) | copy-start | bytes 2949124
  89.7 1.3 copy-start
  91.0 1.0 copy-start.2
  305.6 1.6 copy-start.3
  307.5 1.0 copy-start.4
Sparse Core Ops, SparseCore 0:
  8.9 71.2 all-gather.3
  96.4 195.1 all-gather.5
